TPU v7x, 256 devices: a whole 4x4x8 slice. The times are simulated.
256 devices in a mesh: dp: 64 (over y, z, core), tensor: 4 (over x).
Axes of the slice: x: 4, y: 4, z: 8, core: 2. Of those that a mesh axis runs over, the one named last changes fastest.
Arguments:
- activations: bfloat16 [32768, 8192], P('dp', 'tensor'), may hold values from -2000 to 2000
- norm_gain: float32 [8192], replicated, may hold values from 0.5 to 12
- w_query: bfloat16 [8192, 4096], P('dp', 'tensor'), may hold values from -0.0625 to 0.0625
- w_key: bfloat16 [8192, 512], P('dp', 'tensor'), may hold values from -0.0625 to 0.0625
- w_value: bfloat16 [8192, 512], P('dp', 'tensor'), may hold values from -0.0625 to 0.0625
- lengths: int32 [128], replicated, may hold values from 128 to 256
- languages: int32 [128], replicated, may hold values from 0 to 29
- lang_caps: int32 [30], replicated, may hold values from 128 to 256
- dest_shard: int32 [128], replicated, may hold values from 0 to 63, as said below
Outputs:
- attended: bfloat16 [32768, 4096], P('dp', 'tensor')
Inputs may be any that keep to these rules, and one draw needn't show every extreme that they name: `dest_shard`: every data shard receives exactly 2 documents.
All inputs are finite; a program needn't handle non-finite values.
Results may differ from a plain program's by a relative error of at most 0.007.
The roundings to bfloat16 on the way count: a program that leaves them out, or rounds other values in their place, can miss the bound.
Values may be sent and summed in bfloat16 or wider, within the bound.
A program may use at most 128 MiB of HBM per device.

v0:
```python
import math
import jax
import jax.numpy as jnp
from jax import lax
from jax.sharding import PartitionSpec as P

HEAD_WIDTH = 128
rope_base = 500000.0
norm_eps = 1e-05


def rotary_embedding(vectors, token_positions):
    half_width = vectors.shape[-1] // 2
    steps_range = jnp.arange(half_width, dtype=jnp.float32)
    frequency = jnp.exp(steps_range * (-2.0 * math.log(rope_base) / vectors.shape[-1]))
    angles = token_positions[..., None, None] * frequency
    cosine = jnp.cos(angles)
    sine_table = jnp.sin(angles)
    first_half = vectors[..., :half_width]
    second_half = vectors[..., half_width:]
    return jnp.concatenate(
        [
            first_half * cosine - second_half * sine_table,
            second_half * cosine + first_half * sine_table,
        ],
        axis=-1,
    )


def project(source_rows, norm_gain, w_query, w_key, w_value):
    packed_weight = jnp.concatenate([w_query, w_key, w_value], axis=1)
    weight = lax.all_gather(packed_weight, "dp", axis=0, tiled=True)
    gathered = lax.all_gather(source_rows, "tensor", axis=1, tiled=True)
    widened = gathered.astype(jnp.float32)
    row_scale = lax.rsqrt(jnp.mean(widened * widened, axis=1, keepdims=True) + norm_eps)
    normed = (widened * row_scale * norm_gain).astype(jnp.bfloat16)
    return jnp.dot(normed, weight, preferred_element_type=jnp.float32)


def rotate_round(projected, token_positions, rotated_width, head_dim):
    total_rows = projected.shape[0]
    rotated = rotary_embedding(
        projected[:, :rotated_width].reshape(total_rows, -1, head_dim), token_positions
    ).reshape(total_rows, -1)
    return jnp.concatenate([rotated, projected[:, rotated_width:]], axis=1).astype(jnp.bfloat16)


def attend(packed, doc_lengths, query_width, key_width, head_dim, doc_max):
    total_rows = packed.shape[0]
    doc_total = total_rows // doc_max
    value_head_rows = key_width // head_dim
    heads_per_group = query_width // key_width
    queries = packed[:, :query_width].reshape(
        doc_total, doc_max, value_head_rows, heads_per_group, head_dim
    )
    key_rows = packed[:, query_width : query_width + key_width].reshape(
        doc_total, doc_max, value_head_rows, head_dim
    )
    value_rows = packed[:, query_width + key_width :].reshape(
        doc_total, doc_max, value_head_rows, head_dim
    )
    scores = jnp.einsum(
        "jqhgd,jkhd->jhgqk", queries, key_rows, preferred_element_type=jnp.float32
    ) / math.sqrt(head_dim)
    order_range = jnp.arange(doc_max)
    causal = order_range[:, None] >= order_range[None, :]
    scores = jnp.where(causal, scores, -jnp.inf)
    row_peak = jnp.max(scores, axis=-1, keepdims=True)
    exponent = jnp.exp(scores - row_peak)
    probability = (exponent / jnp.sum(exponent, axis=-1, keepdims=True)).astype(jnp.bfloat16)
    blended = jnp.einsum(
        "jhgqk,jkhd->jqhgd", probability, value_rows, preferred_element_type=jnp.float32
    )
    blended = blended.reshape(doc_total, doc_max, query_width)
    row_valid = order_range[None, :] < doc_lengths[:, None]
    result = jnp.where(row_valid[..., None], blended, 0.0)
    return result.reshape(total_rows, query_width).astype(jnp.bfloat16)


def local(
    activations, norm_gain, w_query, w_key, w_value, lengths, languages, lang_caps, dest_shard
):
    shard_count = lax.axis_size("dp")
    my_shard = lax.axis_index("dp")
    doc_count = lengths.shape[0]
    token_rows = activations.shape[0]
    rows_peer = token_rows // doc_count
    doc_max = rows_peer * shard_count
    docs_here = doc_count // shard_count
    head_dim = HEAD_WIDTH
    query_width = w_query.shape[1]
    key_width = w_key.shape[1]
    language_table = jnp.arange(lang_caps.shape[0])
    cap_of_doc = jnp.sum(
        jnp.where(languages[:, None] == language_table[None, :], lang_caps[None, :], 0), axis=1
    )
    capped = jnp.minimum(lengths, cap_of_doc)
    doc_order = jnp.arange(doc_count)
    same_dest = dest_shard[:, None] == dest_shard[None, :]
    doc_rank = jnp.sum(
        (same_dest & (doc_order[None, :] < doc_order[:, None])).astype(jnp.int32), axis=1
    )
    target_slot = dest_shard * docs_here + doc_rank
    holder = jnp.sum(
        jnp.where(doc_order[:, None] == target_slot[None, :], doc_order[None, :], 0), axis=1
    )
    mine = lax.dynamic_slice_in_dim(holder, my_shard * docs_here, docs_here)
    doc_lengths = jnp.take(capped, mine)
    holder_grid = jnp.transpose(holder.reshape(shard_count, docs_here))
    send_index = (
        holder_grid[:, None, :] * rows_peer + jnp.arange(rows_peer)[None, :, None]
    ).reshape(-1)
    token_positions = (my_shard + shard_count * (jnp.arange(token_rows) % rows_peer)).astype(
        jnp.float32
    )
    projected = project(activations, norm_gain, w_query, w_key, w_value)
    packed = rotate_round(projected, token_positions, query_width + key_width, head_dim)
    outgoing = jnp.take(packed, send_index, axis=0, mode="clip").reshape(
        docs_here, rows_peer, shard_count, -1
    )
    arrived = lax.all_to_all(outgoing, "dp", split_axis=2, concat_axis=2, tiled=True)
    moved_rows = arrived.reshape(docs_here * doc_max, -1)
    return attend(moved_rows, doc_lengths, query_width, key_width, head_dim, doc_max)


def solution(mesh):
    return jax.shard_map(
        local,
        mesh=mesh,
        in_specs=(
            P("dp", "tensor"),
            P(),
            P("dp", "tensor"),
            P("dp", "tensor"),
            P("dp", "tensor"),
            P(),
            P(),
            P(),
            P(),
        ),
        out_specs=P("dp", "tensor"),
        check_vma=False,
    )
```

profile of v0, /device:TPU:1, one launch (start us, length us, event | category | flops | bytes accessed | tf_op | source)
XLA Modules:
  0.0 293.0 jit_solution(14304292000981293359)
XLA Ops:
  6.5 0.7 all-gather.3.cloned.1.call-update
  7.3 1.7 pad_maximum_fusion.2
  9.1 0.2 convert_reduce_fusion
  9.3 0.1 select_reduce_fusion
  9.4 0.1 mul.133
  9.6 0.1 reshape.215
  9.7 0.5 multiply_cosine_fusion
  10.3 88.1 %all-gather.3.cloned.1.call-done = bf16[512,8192]{1,0:T(8,128)(2,1)} async-done(((bf16[512,2048]{1,0:T(8,128)(2,1)}), bf16[512,8192]{1,0:T(8,128)(2,1)}) %all-gather.3.cloned.1.call-update) | async-done | bytes 8388624 | tf_op jit(solution)/shard_map/all_gather | solution.py:33
  98.4 5.1 %fusion = f32[512]{0:T(512)S(1)} fusion(bf16[512,8192]{1,0:T(8,128)(2,1)} %all-gather.3.cloned.1.call-done), kind=kLoop, calls=%fused_computation.4 | loop fusion | flops 12582400 | bytes 8390656 | tf_op jit(solution)/shard_map/reduce_sum | solution.py:35
  103.5 109.2 %all-gather.5.cloned.1.call-done = bf16[8192,1280]{1,0:T(8,128)(2,1)} async-done(((bf16[128,1280]{1,0:T(8,128)(2,1)}), bf16[8192,1280]{1,0:T(8,128)(2,1)}) %all-gather.5.cloned.1.call-update) | async-done | bytes 20971536 | tf_op jit(solution)/shard_map/all_gather | solution.py:32
  212.7 16.5 %fusion.3 = f32[512,1280]{1,0:T(8,128)S(1)} fusion(bf16[8192,1280]{1,0:T(8,128)(2,1)} %all-gather.5.cloned.1.call-done, bf16[512,8192]{1,0:T(8,128)(2,1)} %all-gather.3.cloned.1.call-done, f32[8192]{0:T(1024)S(1)} %copy-done, f32[512]{0:T(512)S(1)} %add_rsqrt_fusion), kind=kOutput, calls=%fused_computation.7 | convolution fusion | flops 10754195456 | bytes 32016384 | tf_op jit(solution)/shard_map/dot_general | solution.py:37
  229.3 1.6 slice.33
  230.9 2.0 copy.28
  232.9 0.4 subtract_convert_fusion
  233.4 1.4 copy.29
  234.8 1.4 pad_maximum_fusion
  236.2 2.1 gather_fusion.1
  238.4 2.1 copy.31
  240.4 6.0 %all-to-all-start = ((bf16[2,4,64,1280]{3,1,0,2:T(4,128)(2,1)}), bf16[2,4,64,1280]{3,1,0,2:T(4,128)(2,1)S(1)}, u32[]{:S(2)}, u32[]{:S(2)}) async-start(bf16[2,4,64,1280]{3,1,0,2:T(4,128)(2,1)} %copy.31), calls=%async_computation | async-start | bytes 2621440 | tf_op jit(solution)/shard_map/all_to_all | solution.py:121
  246.4 0.1 select_reduce_fusion.1
  246.5 0.1 compare_select_fusion
  246.6 0.6 gather_fusion
  247.3 0.1 and_select_fusion
  247.5 33.1 %all-to-all-done = bf16[2,4,64,1280]{3,1,0,2:T(4,128)(2,1)S(1)} async-done(((bf16[2,4,64,1280]{3,1,0,2:T(4,128)(2,1)}), bf16[2,4,64,1280]{3,1,0,2:T(4,128)(2,1)S(1)}, u32[]{:S(2)}, u32[]{:S(2)}) %all-to-all-start) | async-done | bytes 1310752 | tf_op jit(solution)/shard_map/all_to_all | solution.py:121
  280.5 0.2 copy.32
  280.8 0.1 slice_bitcast_fusion
  280.9 0.3 copy.42
  281.2 0.8 fusion.8
  282.0 0.9 fusion.7
  282.9 1.3 fusion.13
  284.2 0.8 copy.36
  284.9 1.2 fusion.9
  (29 shorter events, 0.5 us)
Async XLA Ops:
  6.5 2.5 copy-start.1
  6.5 91.9 %all-gather.3.cloned.1.call-start = ((), (), s32[]{:S(2)}) async-start(), calls=%async_computation.1 | async-start | bytes 10485760 | tf_op jit(solution)/shard_map/all_gather | solution.py:33
  7.3 205.5 %all-gather.5.cloned.1.call-start = ((), (), s32[]{:S(2)}) async-start(), calls=%async_computation.2 | async-start | bytes 21299200 | tf_op jit(solution)/shard_map/all_gather | solution.py:32
  10.3 202.4 %copy-start = (f32[8192]{0:T(1024)S(1)}, f32[8192]{0:T(1024)}, u32[]{:S(2)}) copy-start(f32[8192]{0:T(1024)} %param.10) | copy-start | bytes 98308
  238.3 8.1 %copy-start.2 = (s32[30]{0:T(128)S(1)}, s32[30]{0:T(128)}, u32[]{:S(2)}) copy-start(s32[30]{0:T(128)} %param.16) | copy-start | bytes 364
  238.3 8.1 %copy-start.3 = (s32[128]{0:T(128)S(1)}, s32[128]{0:T(128)}, u32[]{:S(2)}) copy-start(s32[128]{0:T(128)} %param.15) | copy-start | bytes 1540
  238.3 8.2 %copy-start.4 = (s32[128]{0:T(128)S(1)}, s32[128]{0:T(128)}, u32[]{:S(2)}) copy-start(s32[128]{0:T(128)} %param.14) | copy-start | bytes 1540
  240.4 40.1 %all-to-all-start = ((bf16[2,4,64,1280]{3,1,0,2:T(4,128)(2,1)}), bf16[2,4,64,1280]{3,1,0,2:T(4,128)(2,1)S(1)}, u32[]{:S(2)}, u32[]{:S(2)}) async-start(bf16[2,4,64,1280]{3,1,0,2:T(4,128)(2,1)} %copy.31), calls=%async_computation | async-start | bytes 2621440 | tf_op jit(solution)/shard_map/all_to_all | solution.py:121
Sparse Core Ops, SparseCore 0:
  9.1 89.2 all-gather.2
  101.1 111.5 all-gather.4
where the time goes:
time: 293 us
  waiting for transfers between devices  231 us (79%)
  matrix products  18.6 us (6%)
  between operations  13.6 us (5%)
  other arithmetic  12 us (4%)
  local copies, waits for them, and re-layouts  11.6 us (4%)
  starting transfers between devices  6.01 us (2%)
    all_gather x1, waiting for transfers between devices, project(): weight = lax.all_gather(packed_weight, 'dp', axis=0, tiled=True)  109 us
    all_gather x1, waiting for transfers between devices, project(): gathered = lax.all_gather(source_rows, 'tensor', axis=1, tiled=True)  88.1 us
    all_to_all x1, waiting for transfers between devices, local(): lax.all_to_all(outgoing, 'dp', split_axis=2, concat_axis=2, tiled=True)  33.1 us
    dot_general x1, matrix products, project(): return jnp.dot(normed, weight, preferred_element_type=jnp.float32)  16.5 us
    all_to_all x1, starting transfers between devices, local(): lax.all_to_all(outgoing, 'dp', split_axis=2, concat_axis=2, tiled=True)  5.97 us
  transfers between devices with their start and end apart: 3, of which 3 were waited for; matrix products, arithmetic and copies ran while one was open for 3% of the time, Pallas kernels for 0%

commit v1 on v0

--- a/solution.py
+++ b/solution.py
@@ -7,6 +7,28 @@
 HEAD_WIDTH = 128
 rope_base = 500000.0
 norm_eps = 1e-05
+
+
+def laid_out(blocks, dim):
+    shape = list(blocks.shape[1:])
+    shape[dim] *= blocks.shape[0]
+    return jnp.moveaxis(blocks, 0, dim).reshape(shape)
+
+
+def collect(x, axis, dim):
+    devices = lax.axis_size(axis)
+    pairs = [(i, (i + 1) % devices) for i in range(devices)]
+    back = [(b, a) for a, b in pairs]
+    lower, upper = ([], [])
+    for step in range(devices - 1):
+        if step % 2 == 0:
+            lower.append(lax.ppermute(lower[-1] if lower else x, axis, pairs))
+        else:
+            upper.append(lax.ppermute(upper[-1] if upper else x, axis, back))
+    tiles = jnp.stack([*lower[::-1], x, *upper])
+    shift = lax.axis_index(axis) - len(lower)
+    tiles = tiles[(jnp.arange(devices) - shift) % devices]
+    return laid_out(tiles, dim)
 
 
 def rotary_embedding(vectors, token_positions):
@@ -30,7 +52,7 @@
 def project(source_rows, norm_gain, w_query, w_key, w_value):
     packed_weight = jnp.concatenate([w_query, w_key, w_value], axis=1)
     weight = lax.all_gather(packed_weight, "dp", axis=0, tiled=True)
-    gathered = lax.all_gather(source_rows, "tensor", axis=1, tiled=True)
+    gathered = collect(source_rows, "tensor", 1)
     widened = gathered.astype(jnp.float32)
     row_scale = lax.rsqrt(jnp.mean(widened * widened, axis=1, keepdims=True) + norm_eps)
     normed = (widened * row_scale * norm_gain).astype(jnp.bfloat16)

time: 293 us -> 252 us (0.86)
  waiting for transfers between devices: 231 us -> 119 us
  local copies, waits for them, and re-layouts: 11.6 us -> 41.5 us
  other arithmetic: 12 us -> 36.7 us
  starting transfers between devices: 6.01 us -> 21.4 us
    all_gather x1, waiting for transfers between devices: 109 us -> 0.01 us  [project(): weight = lax.all_gather(packed_weight, 'dp', axis=0, tiled=True)]
    all_gather x1 -> x0, waiting for transfers between devices: 88.1 us -> none  [project(): gathered = lax.all_gather(source_rows, 'tensor', axis=1, tiled=True)]
    ppermute x0 -> x3, waiting for transfers between devices: none -> 85.4 us  [the longest x2 85.4 us: collect(): lower.append(lax.ppermute(lower[-1] if lower else x, axis, pairs))]
    convert_element_type x0 -> x2, other arithmetic: none -> 20.8 us  [the longest x1 11.6 us: project(): widened = gathered.astype(jnp.float32)]
    convert_element_type x0 -> x1, local copies, waits for them, and re-layouts: none -> 16.4 us  [project(): widened = gathered.astype(jnp.float32)]
    gather x0 -> x3, local copies, waits for them, and re-layouts: none -> 14 us  [collect(): tiles = tiles[(jnp.arange(devices) - shift) % devices]]
    all_to_all x1, starting transfers between devices: 5.97 us -> 16.1 us  [local(): lax.all_to_all(outgoing, 'dp', split_axis=2, concat_axis=2, tiled=True)]
    ppermute x0 -> x3, starting transfers between devices: none -> 5.33 us  [the longest x2 3.97 us: collect(): lower.append(lax.ppermute(lower[-1] if lower else x, axis, pairs))]
  transfers between devices with their start and end apart: 3 -> 5, of which waited for: 3 -> 3; matrix products, arithmetic and copies ran while one was open for 3% -> 25% of each run, Pallas kernels for 0% -> 0%
where the time goes in v1:
time: 252 us; the launch traced here: 251 us
  waiting for transfers between devices  119 us (47%)
  local copies, waits for them, and re-layouts  41.5 us (16%)
  other arithmetic  36.7 us (15%)
  starting transfers between devices  21.4 us (8%)
  matrix products  19.1 us (8%)
  between operations  13.7 us (5%)
    ppermute x2, waiting for transfers between devices, collect(): lower.append(lax.ppermute(lower[-1] if lower else x, axis, pairs))  85.4 us
    all_to_all x1, waiting for transfers between devices, local(): lax.all_to_all(outgoing, 'dp', split_axis=2, concat_axis=2, tiled=True)  33.1 us
    dot_general x1, matrix products, project(): return jnp.dot(normed, weight, preferred_element_type=jnp.float32)  17 us
    convert_element_type x1, local copies, waits for them, and re-layouts, project(): widened = gathered.astype(jnp.float32)  16.4 us
    all_to_all x1, starting transfers between devices, local(): lax.all_to_all(outgoing, 'dp', split_axis=2, concat_axis=2, tiled=True)  16.1 us
    gather x3, local copies, waits for them, and re-layouts, collect(): tiles = tiles[(jnp.arange(devices) - shift) % devices]  14 us
    convert_element_type x1, other arithmetic, project(): widened = gathered.astype(jnp.float32)  11.6 us
    convert_element_type x1, other arithmetic, project(): normed = (widened * row_scale * norm_gain).astype(jnp.bfloat16)  9.25 us
  transfers between devices with their start and end apart: 5, of which 3 were waited for; matrix products, arithmetic and copies ran while one was open for 25% of the time, Pallas kernels for 0%

profile of v1, /device:TPU:1, one launch (start us, length us, event | category | flops | bytes accessed | tf_op | source)
XLA Modules:
  0.0 250.9 jit_solution(5960612333627656045)
XLA Ops:
  6.5 1.7 pad_maximum_fusion.4
  8.3 2.1 collective-permute-start
  10.4 1.4 collective-permute-start.2
  11.8 43.4 %collective-permute-done = bf16[512,2048]{1,0:T(8,128)(2,1)S(1)} collective-permute-done((bf16[512,2048]{1,0:T(8,128)(2,1)}, bf16[512,2048]{1,0:T(8,128)(2,1)S(1)}, u32[]{:S(2)}, u32[]{:S(2)}) %collective-permute-start) | collective-permute-done | bytes 2097184 | tf_op jit(solution)/shard_map/ppermute | solution.py:25
  55.1 1.9 collective-permute-start.1
  57.0 0.9 convert_reduce_fusion
  57.9 0.7 multiply_add_fusion
  59.1 0.5 multiply_cosine_fusion
  59.6 42.0 %collective-permute-done.1 = bf16[512,2048]{1,0:T(8,128)(2,1)} collective-permute-done((bf16[512,2048]{1,0:T(8,128)(2,1)S(1)}, bf16[512,2048]{1,0:T(8,128)(2,1)}, u32[]{:S(2)}, u32[]{:S(2)}) %collective-permute-start.1) | collective-permute-done | bytes 2097184 | tf_op jit(solution)/shard_map/ppermute | solution.py:25
  101.7 4.0 %pad_maximum_fusion = bf16[4,512,2048]{2,1,0:T(8,128)(2,1)S(1)} fusion(bf16[1,512,2048]{2,1,0:T(8,128)(2,1)} %bitcast.3, bf16[1,512,2048]{2,1,0:T(8,128)(2,1)} %bitcast.75, bf16[1,512,2048]{2,1,0:T(8,128)(2,1)S(1)} %bitcast.76, bf16[1,512,2048]{2,1,0:T(8,128)(2,1)} %bitcast), kind=kLoop, calls=%fused_computation.10 | loop fusion | flops 12582912 | bytes 16777216 | tf_op jit(solution)/shard_map/stack | solution.py:28
  105.7 3.9 %fusion.25 = (bf16[4,512,1024]{2,1,0:T(8,128)(2,1)}, bf16[4,512,1024]{2,1,0:T(8,128)(2,1)}) fusion(bf16[4,512,2048]{2,1,0:T(8,128)(2,1)S(1)} %pad_maximum_fusion), kind=kLoop, calls=%fused_computation.69 | loop fusion | bytes 16777216 | tf_op jit(solution)/shard_map/gather | solution.py:30
  109.6 5.1 %gather_fusion.2 = bf16[4,512,1024]{2,1,0:T(8,128)(2,1)} fusion(bf16[4,512,1024]{2,1,0:T(8,128)(2,1)} %get-tuple-element.5, s32[1024]{0:T(1024)S(1)} %pad_clamp_fusion.1), kind=kCustom, calls=%fused_computation.2 | custom fusion | bytes 8388624 | tf_op jit(solution)/shard_map/gather | solution.py:30
  114.7 5.1 %gather_fusion.3 = bf16[4,512,1024]{2,1,0:T(8,128)(2,1)} fusion(bf16[4,512,1024]{2,1,0:T(8,128)(2,1)} %get-tuple-element.6, s32[1024]{0:T(1024)S(1)} %pad_clamp_fusion.1), kind=kCustom, calls=%fused_computation.3 | custom fusion | bytes 8388624 | tf_op jit(solution)/shard_map/gather | solution.py:30
  119.7 11.6 %convert_bitcast_fusion = f32[512,4,2048]{2,0,1:T(8,128)} fusion(bf16[4,512,1024]{2,1,0:T(8,128)(2,1)} %gather_fusion.3, bf16[4,512,1024]{2,1,0:T(8,128)(2,1)} %gather_fusion.2), kind=kLoop, calls=%fused_computation.5 | loop fusion | flops 16777216 | bytes 25165824 | tf_op jit(solution)/shard_map/convert_element_type | solution.py:56
  131.3 16.4 %copy.37 = f32[512,4,2048]{0,2,1:T(8,128)} copy(f32[512,4,2048]{2,0,1:T(8,128)} %convert_bitcast_fusion) | data formatting | bytes 33554432 | tf_op jit(solution)/shard_map/convert_element_type | solution.py:56
  147.6 4.9 %fusion = f32[512]{0:T(512)S(1)} fusion(bf16[4,512,1024]{2,1,0:T(8,128)(2,1)} %gather_fusion.3, bf16[4,512,1024]{2,1,0:T(8,128)(2,1)} %gather_fusion.2), kind=kLoop, calls=%fused_computation.6 | loop fusion | flops 25165312 | bytes 8390656 | tf_op jit(solution)/shard_map/reduce_sum | solution.py:57
  152.5 9.3 %fusion.2 = bf16[512,8192]{0,1:T(8,128)(2,1)} fusion(f32[512,4,2048]{0,2,1:T(8,128)} %copy.37, f32[8192]{0:T(1024)S(1)} %copy-done, f32[512]{0:T(512)S(1)} %add_rsqrt_fusion), kind=kLoop, calls=%fused_computation.9 | loop fusion | flops 12582912 | bytes 25200640 | tf_op jit(solution)/shard_map/convert_element_type | solution.py:58
  161.8 17.0 %fusion.27 = f32[512,1280]{1,0:T(8,128)S(1)} fusion(bf16[512,8192]{0,1:T(8,128)(2,1)} %fusion.2, bf16[8192,1280]{1,0:T(8,128)(2,1)} %all-gather.2.cloned.1.call-done), kind=kOutput, calls=%fused_computation.71 | convolution fusion | flops 10737418240 | bytes 31981568 | tf_op jit(solution)/shard_map/dot_general | solution.py:59
  178.8 1.6 slice.37
  180.4 2.0 copy.38
  182.4 0.4 subtract_convert_fusion
  182.9 0.7 copy.39
  183.8 2.4 gather_fusion.1
  186.2 2.1 copy.41
  188.2 16.1 %all-to-all-start = ((bf16[2,4,64,1280]{3,1,0,2:T(4,128)(2,1)}), bf16[2,4,64,1280]{3,1,0,2:T(4,128)(2,1)S(1)}, u32[]{:S(2)}, u32[]{:S(2)}) async-start(bf16[2,4,64,1280]{3,1,0,2:T(4,128)(2,1)} %copy.41), calls=%async_computation | async-start | bytes 2621440 | tf_op jit(solution)/shard_map/all_to_all | solution.py:143
  204.5 0.6 gather_fusion
  205.4 33.1 %all-to-all-done = bf16[2,4,64,1280]{3,1,0,2:T(4,128)(2,1)S(1)} async-done(((bf16[2,4,64,1280]{3,1,0,2:T(4,128)(2,1)}), bf16[2,4,64,1280]{3,1,0,2:T(4,128)(2,1)S(1)}, u32[]{:S(2)}, u32[]{:S(2)}) %all-to-all-start) | async-done | bytes 1310752 | tf_op jit(solution)/shard_map/all_to_all | solution.py:143
  239.1 0.8 fusion.4
  239.9 0.9 fusion.3
  240.8 1.3 fusion.9
  242.1 0.8 copy.46
  242.9 1.2 fusion.5
  (39 shorter events, 1.7 us)
Async XLA Ops:
  6.5 155.3 %all-gather.2.cloned.1.call-start = ((), (), s32[]{:S(2)}) async-start(), calls=%async_computation.1 | async-start | bytes 21299200 | tf_op jit(solution)/shard_map/all_gather | solution.py:54
  8.3 46.8 %collective-permute-start = (bf16[512,2048]{1,0:T(8,128)(2,1)}, bf16[512,2048]{1,0:T(8,128)(2,1)S(1)}, u32[]{:S(2)}, u32[]{:S(2)}) collective-permute-start(bf16[512,2048]{1,0:T(8,128)(2,1)} %param.9), channel_id=1, source_target_pairs={{0,1},{1,2},{2,3},{3,0},{4,5},{5,6},{6,7},{7,4},{8,9},{9,10},{10,1... | collective-permute-start | bytes 6291464 | tf_op jit(solution)/shard_map/ppermute | solution.py:25
  10.4 49.2 %collective-permute-start.2 = (bf16[512,2048]{1,0:T(8,128)(2,1)}, bf16[512,2048]{1,0:T(8,128)(2,1)}, u32[]{:S(2)}, u32[]{:S(2)}) collective-permute-start(bf16[512,2048]{1,0:T(8,128)(2,1)} %param.9), channel_id=1, source_target_pairs={{1,0},{2,1},{3,2},{0,3},{5,4},{6,5},{7,6},{4,7},{9,8},{10,9},{11,1... | collective-permute-start | bytes 6291464 | tf_op jit(solution)/shard_map/ppermute | solution.py:27
  55.1 46.5 %collective-permute-start.1 = (bf16[512,2048]{1,0:T(8,128)(2,1)S(1)}, bf16[512,2048]{1,0:T(8,128)(2,1)}, u32[]{:S(2)}, u32[]{:S(2)}) collective-permute-start(bf16[512,2048]{1,0:T(8,128)(2,1)S(1)} %collective-permute-done), channel_id=1, source_target_pairs={{0,1},{1,2},{2,3},{3,0},{4,5},{5,6},{6,7},{7,4},{8,9},{9,10},{10,1... | collective-permute-start | bytes 6291464 | tf_op jit(solution)/shard_map/ppermute | solution.py:25
  147.6 4.9 %copy-start = (f32[8192]{0:T(1024)S(1)}, f32[8192]{0:T(1024)}, u32[]{:S(2)}) copy-start(f32[8192]{0:T(1024)} %param.10) | copy-start | bytes 98308
  186.1 18.2 %copy-start.1 = (s32[30]{0:T(128)S(1)}, s32[30]{0:T(128)}, u32[]{:S(2)}) copy-start(s32[30]{0:T(128)} %param.16) | copy-start | bytes 364
  186.1 18.2 %copy-start.2 = (s32[128]{0:T(128)S(1)}, s32[128]{0:T(128)}, u32[]{:S(2)}) copy-start(s32[128]{0:T(128)} %param.15) | copy-start | bytes 1540
  186.1 18.3 %copy-start.3 = (s32[128]{0:T(128)S(1)}, s32[128]{0:T(128)}, u32[]{:S(2)}) copy-start(s32[128]{0:T(128)} %param.14) | copy-start | bytes 1540
  188.2 50.2 %all-to-all-start = ((bf16[2,4,64,1280]{3,1,0,2:T(4,128)(2,1)}), bf16[2,4,64,1280]{3,1,0,2:T(4,128)(2,1)S(1)}, u32[]{:S(2)}, u32[]{:S(2)}) async-start(bf16[2,4,64,1280]{3,1,0,2:T(4,128)(2,1)} %copy.41), calls=%async_computation | async-start | bytes 2621440 | tf_op jit(solution)/shard_map/all_to_all | solution.py:143
Sparse Core Ops, SparseCore 0:
  10.1 114.1 all-gather.1
